TPU v7x, 32 devices: a whole 2x2x4 slice. The times are simulated.
32 devices in a mesh: frames: 8 (over y, x, core), rows: 4 (over z).
Axes of the slice: x: 2, y: 2, z: 4, core: 2. Of those that a mesh axis runs over, the one named last changes fastest.
Arguments:
- video: bfloat16 [8, 16, 320, 192], P('frames', 'rows'), may hold values from -6 to 6
- spatial_weights: bfloat16 [4, 3, 3, 192, 192], replicated, may hold values from -0.15625 to 0.15625
- norm_gains: float32 [4, 192], replicated, may hold values from 0.5 to 1.5
- temporal_weights: bfloat16 [2, 3, 192, 192], replicated, may hold values from -0.25 to 0.25
Outputs:
- decoded: bfloat16 [8, 16, 320, 192], P('frames', 'rows')
All inputs are finite; a program needn't handle non-finite values.
Results may differ from a plain program's by a relative error of at most 0.013.
Values may be sent and summed in bfloat16 or wider, within the bound.
A program may use at most 64 MiB of HBM per device.

v0:
```python
import jax
import jax.numpy as jnp
from jax import lax
from jax.sharding import PartitionSpec as P

epsilon = 1e-06


def shifted(block, axis, distance):
    devices = range(lax.axis_size(axis))
    route = [(i - distance, i) for i in devices if i - distance in devices]
    return lax.ppermute(block, axis, route)


def extended_2(cells, sides, width):
    for axis, dim in sides:
        count = lax.axis_size(axis)
        ends = count - 1
        head = lax.slice_in_dim(cells, 0, width, axis=dim)
        tail = lax.slice_in_dim(cells, cells.shape[dim] - width, cells.shape[dim], axis=dim)
        cells = jnp.concatenate(
            [
                lax.ppermute(tail, axis, [(i, (i + 1) % count) for i in range(ends)]),
                cells,
                lax.ppermute(head, axis, [((i + 1) % count, i) for i in range(ends)]),
            ],
            axis=dim,
        )
    return cells


def activate(values, gain):
    values = values.astype(jnp.float32)
    mean_sq = jnp.mean(values * values, axis=-1, keepdims=True)
    scaled = values * lax.rsqrt(mean_sq + epsilon) * gain
    return jax.nn.silu(scaled).astype(jnp.bfloat16)


def convolve(active, kernel):
    out_rows = active.shape[1] - 2
    width = active.shape[2]
    padded = jnp.pad(active, ((0, 0), (0, 0), (1, 1), (0, 0)))
    total = None
    for row_step in range(3):
        for col_step in range(3):
            window = padded[:, row_step : row_step + out_rows, col_step : col_step + width]
            term = jnp.einsum(
                "frwc,cd->frwd",
                window,
                kernel[row_step, col_step],
                preferred_element_type=jnp.float32,
            )
            total = term if total is None else total + term
    return total


def past_frames(inner):
    frame_count = inner.shape[0]
    hops = (frame_count + 1) // frame_count
    pieces = []
    for offset in range(1, hops + 1):
        pieces.append(shifted(inner, "frames", offset))
    joined = jnp.concatenate(pieces[::-1], axis=0)
    return joined


def on_device(video, spatial_weights, norm_gains, temporal_weights):
    current = video
    frame_count = video.shape[0]
    rows_dev = video.shape[1]
    first_row = lax.axis_index("rows") * rows_dev
    all_rows = rows_dev * lax.axis_size("rows")
    for block in range(spatial_weights.shape[0] // 2):
        widened = extended_2(current, (("rows", 1),), 2)
        first = convolve(activate(widened, norm_gains[2 * block]), spatial_weights[2 * block])
        row_index = first_row - 1 + jnp.arange(rows_dev + 2, dtype=jnp.int32)
        inside = (row_index >= 0) & (row_index < all_rows)
        first = jnp.where(inside[None, :, None, None], first, 0.0).astype(jnp.bfloat16)
        second = convolve(
            activate(first, norm_gains[2 * block + 1]), spatial_weights[2 * block + 1]
        )
        inner = (current.astype(jnp.float32) + second).astype(jnp.bfloat16)
        history = past_frames(inner)
        extended = jnp.concatenate([history, inner], axis=0)
        total = inner.astype(jnp.float32)
        for offset in range(3):
            frames_in = extended[2 - offset : 2 - offset + frame_count]
            total = total + jnp.einsum(
                "frwc,cd->frwd",
                frames_in,
                temporal_weights[block, offset],
                preferred_element_type=jnp.float32,
            )
        current = total.astype(jnp.bfloat16)
    return current


def solution(mesh):
    placed = (P("frames", "rows", None, None), P(), P(), P())
    return jax.shard_map(
        on_device,
        mesh=mesh,
        in_specs=placed,
        out_specs=P("frames", "rows", None, None),
        check_vma=False,
    )
```

profile of v0, /device:TPU:20, one launch (start us, length us, event | category | flops | bytes accessed | tf_op | source)
XLA Modules:
  0.0 99.0 jit_solution(7805967008355556469)
XLA Ops:
  0.0 1.9 %fusion.182 = (bf16[1,2,320,192]{2,3,1,0:T(8,128)(2,1)}, bf16[1,2,320,192]{2,3,1,0:T(8,128)(2,1)}) fusion(bf16[1,4,320,192]{2,3,1,0:T(8,128)(2,1)} %param.4), kind=kLoop, calls=%fused_computation.268 | loop fusion | bytes 983040 | tf_op jit(solution)/shard_map/slice | solution.py:20
  1.9 3.5 %collective-permute-start = (bf16[1,2,320,192]{2,3,1,0:T(8,128)(2,1)}, bf16[1,2,320,192]{2,3,1,0:T(8,128)(2,1)S(1)}, u32[]{:S(2)}, u32[]{:S(2)}) collective-permute-start(bf16[1,2,320,192]{2,3,1,0:T(8,128)(2,1)} %get-tuple-element.11), channel_id=1, source_target_pairs={{0,1},{1,2},{2,3},{4,5},{5,6},{6,7},{8,9},{9,10},{10,11},{12,13},{... | collective-permute-start | bytes 737288 | tf_op jit(solution)/shard_map/ppermute | solution.py:23
  5.4 2.4 %collective-permute-start.1 = (bf16[1,2,320,192]{2,3,1,0:T(8,128)(2,1)}, bf16[1,2,320,192]{2,3,1,0:T(8,128)(2,1)}, u32[]{:S(2)}, u32[]{:S(2)}) collective-permute-start(bf16[1,2,320,192]{2,3,1,0:T(8,128)(2,1)} %get-tuple-element.12), channel_id=1, source_target_pairs={{1,0},{2,1},{3,2},{5,4},{6,5},{7,6},{9,8},{10,9},{11,10},{13,12},{... | collective-permute-start | bytes 737288 | tf_op jit(solution)/shard_map/ppermute | solution.py:25
  7.8 3.6 %fusion.180 = (bf16[1,3,3,192,192]{4,3,2,1,0:T(8,128)(2,1)}, bf16[1,3,3,192,192]{4,3,2,1,0:T(8,128)(2,1)S(1)}, bf16[1,3,3,192,192]{4,3,2,1,0:T(8,128)(2,1)}, bf16[1,3,3,192,192]{4,3,2,1,0:T(8,128)(2,1)S(1)}) fusion(bf16[4,3,3,192,192]{4,3,2,1,0:T(8,128)(2,1)} %param.5), kind=kLoop, calls=%fused_computation.266 | loop fusion | bytes 5308416 | tf_op jit(solution)/shard_map/slice | solution.py:80
  11.3 0.8 copy.16
  12.1 1.7 %copy.15 = bf16[1,3,3,192,192]{3,4,2,1,0:T(8,128)(2,1)S(1)} copy(bf16[1,3,3,192,192]{4,3,2,1,0:T(8,128)(2,1)} %get-tuple-element.7) | data formatting | bytes 1327104
  13.8 2.3 %collective-permute-done.1 = bf16[1,2,320,192]{2,3,1,0:T(8,128)(2,1)} collective-permute-done((bf16[1,2,320,192]{2,3,1,0:T(8,128)(2,1)}, bf16[1,2,320,192]{2,3,1,0:T(8,128)(2,1)}, u32[]{:S(2)}, u32[]{:S(2)}) %collective-permute-start.1) | collective-permute-done | bytes 245792 | tf_op jit(solution)/shard_map/ppermute | solution.py:25
  16.1 1.3 %fusion = f32[8,320]{1,0:T(8,128)S(1)} fusion(bf16[1,2,320,192]{2,3,1,0:T(8,128)(2,1)} %collective-permute-done.1, bf16[1,4,320,192]{2,3,1,0:T(8,128)(2,1)S(1)} %copy-done, bf16[1,2,320,192]{2,3,1,0:T(8,128)(2,1)S(1)} %collective-permute-done), kind=kLoop, calls=%fused_computation.4 | loop fusion | flops 2455040 | bytes 993280 | tf_op jit(solution)/shard_map/reduce_sum | solution.py:34
  17.4 1.8 %fusion.7 = bf16[1,8,320,192]{2,3,1,0:T(8,128)(2,1)S(1)} fusion(f32[192]{0:T(256)S(1)} %bitcast.441, f32[8,320]{1,0:T(8,128)S(1)} %add_rsqrt_fusion.3, bf16[1,2,320,192]{2,3,1,0:T(8,128)(2,1)} %collective-permute-done.1, bf16[1,4,320,192]{2,3,1,0:T(8,128)(2,1)S(1)} %copy-done, bf16[1,2,320,192]{2,3,1,0:T(8,128)(2,1)S(1)} %collective-permute-done), kind=kLoop, calls=%fused_computation.11 | loop fusion | flops 4915200 | bytes 1977088 | tf_op jit(solution)/shard_map/convert_element_type | solution.py:36
  19.6 0.5 fusion.64
  20.1 0.5 fusion.66
  21.0 0.5 fusion.68
  21.5 0.5 fusion.70
  22.4 0.5 fusion.72
  22.9 1.2 %fusion.16 = (f32[6,320]{1,0:T(8,128)S(1)}, bf16[6,320,192]{1,2,0:T(8,128)(2,1)S(1)}) fusion(bf16[1,8,320,192]{2,3,1,0:T(8,128)(2,1)S(1)} %fusion.7, bf16[3,3,192,192]{2,3,1,0:T(8,128)(2,1)S(1)} %bitcast.410, f32[6,320,192]{1,2,0:T(8,128)S(1)} %fusion.49, f32[6,320,192]{1,2,0:T(8,128)S(1)} %fusion.64, f32[6,320,192]{1,2,0:T(8,128)S(1)} %fusion.66, ...), kind=kOutput, calls=%fused_computation.24 | convolution fusion | flops 146348160 | bytes 16179200 | tf_op jit(solution)/shard_map/frwc,cd->frwd/dot_general | solution.py:47
  24.1 0.6 fusion.45
  24.8 0.4 fusion.106
  25.5 0.4 convolution_add_fusion.14
  25.9 0.4 convolution_add_fusion.13
  26.7 0.4 convolution_add_fusion.11
  27.8 0.4 fusion.41
  28.3 3.4 %collective-permute-start.3 = (bf16[1,4,320,192]{2,3,1,0:T(8,128)(2,1)S(1)}, bf16[1,4,320,192]{2,3,1,0:T(8,128)(2,1)S(1)}, u32[]{:S(2)}, u32[]{:S(2)}) collective-permute-start(bf16[1,4,320,192]{2,3,1,0:T(8,128)(2,1)S(1)} %fusion.41), channel_id=1, source_target_pairs={{0,8},{4,12},{8,16},{12,20},{16,24},{20,28},{1,9},{5,13},{9,17},{1... | collective-permute-start | bytes 1474568 | tf_op jit(solution)/shard_map/ppermute | solution.py:12
  31.7 1.9 %collective-permute-start.2 = (bf16[1,4,320,192]{2,3,1,0:T(8,128)(2,1)S(1)}, bf16[1,4,320,192]{2,3,1,0:T(8,128)(2,1)S(1)}, u32[]{:S(2)}, u32[]{:S(2)}) collective-permute-start(bf16[1,4,320,192]{2,3,1,0:T(8,128)(2,1)S(1)} %fusion.41), channel_id=1, source_target_pairs={{0,4},{4,8},{8,12},{12,16},{16,20},{20,24},{24,28},{1,5},{5,9},{9,... | collective-permute-start | bytes 1474568 | tf_op jit(solution)/shard_map/ppermute | solution.py:12
  34.0 13.3 %collective-permute-done.3 = bf16[1,4,320,192]{2,3,1,0:T(8,128)(2,1)S(1)} collective-permute-done((bf16[1,4,320,192]{2,3,1,0:T(8,128)(2,1)S(1)}, bf16[1,4,320,192]{2,3,1,0:T(8,128)(2,1)S(1)}, u32[]{:S(2)}, u32[]{:S(2)}) %collective-permute-start.3) | collective-permute-done | bytes 491552 | tf_op jit(solution)/shard_map/ppermute | solution.py:12
  47.6 3.7 %collective-permute-done.2 = bf16[1,4,320,192]{2,3,1,0:T(8,128)(2,1)S(1)} collective-permute-done((bf16[1,4,320,192]{2,3,1,0:T(8,128)(2,1)S(1)}, bf16[1,4,320,192]{2,3,1,0:T(8,128)(2,1)S(1)}, u32[]{:S(2)}, u32[]{:S(2)}) %collective-permute-start.2) | collective-permute-done | bytes 491552 | tf_op jit(solution)/shard_map/ppermute | solution.py:12
  51.7 0.9 fusion.181
  52.6 2.5 %collective-permute-start.4 = (bf16[1,2,320,192]{2,3,1,0:T(8,128)(2,1)}, bf16[1,2,320,192]{2,3,1,0:T(8,128)(2,1)S(1)}, u32[]{:S(2)}, u32[]{:S(2)}) collective-permute-start(bf16[1,2,320,192]{2,3,1,0:T(8,128)(2,1)} %get-tuple-element.9), channel_id=1, source_target_pairs={{0,1},{1,2},{2,3},{4,5},{5,6},{6,7},{8,9},{9,10},{10,11},{12,13},{... | collective-permute-start | bytes 737288 | tf_op jit(solution)/shard_map/ppermute | solution.py:23
  55.1 3.5 %collective-permute-start.5 = (bf16[1,2,320,192]{2,3,1,0:T(8,128)(2,1)}, bf16[1,2,320,192]{2,3,1,0:T(8,128)(2,1)}, u32[]{:S(2)}, u32[]{:S(2)}) collective-permute-start(bf16[1,2,320,192]{2,3,1,0:T(8,128)(2,1)} %get-tuple-element.10), channel_id=1, source_target_pairs={{1,0},{2,1},{3,2},{5,4},{6,5},{7,6},{9,8},{10,9},{11,10},{13,12},{... | collective-permute-start | bytes 737288 | tf_op jit(solution)/shard_map/ppermute | solution.py:25
  58.6 0.8 copy.20
  59.4 0.8 copy.21
  60.1 1.7 %collective-permute-done.4 = bf16[1,2,320,192]{2,3,1,0:T(8,128)(2,1)S(1)} collective-permute-done((bf16[1,2,320,192]{2,3,1,0:T(8,128)(2,1)}, bf16[1,2,320,192]{2,3,1,0:T(8,128)(2,1)S(1)}, u32[]{:S(2)}, u32[]{:S(2)}) %collective-permute-start.4) | collective-permute-done | bytes 245792 | tf_op jit(solution)/shard_map/ppermute | solution.py:23
  61.8 2.4 %collective-permute-done.5 = bf16[1,2,320,192]{2,3,1,0:T(8,128)(2,1)} collective-permute-done((bf16[1,2,320,192]{2,3,1,0:T(8,128)(2,1)}, bf16[1,2,320,192]{2,3,1,0:T(8,128)(2,1)}, u32[]{:S(2)}, u32[]{:S(2)}) %collective-permute-start.5) | collective-permute-done | bytes 245792 | tf_op jit(solution)/shard_map/ppermute | solution.py:25
  64.1 1.3 %fusion.8 = f32[8,320]{1,0:T(8,128)S(1)} fusion(bf16[1,2,320,192]{2,3,1,0:T(8,128)(2,1)} %collective-permute-done.5, bf16[1,4,320,192]{2,3,1,0:T(8,128)(2,1)S(1)} %fusion.43, bf16[1,2,320,192]{2,3,1,0:T(8,128)(2,1)S(1)} %collective-permute-done.4), kind=kLoop, calls=%fused_computation.12 | loop fusion | flops 2455040 | bytes 993280 | tf_op jit(solution)/shard_map/reduce_sum | solution.py:34
  65.4 1.8 %fusion.15 = bf16[1,8,320,192]{2,3,1,0:T(8,128)(2,1)S(1)} fusion(f32[192]{0:T(256)S(1)} %bitcast.439, f32[8,320]{1,0:T(8,128)S(1)} %add_rsqrt_fusion.1, bf16[1,2,320,192]{2,3,1,0:T(8,128)(2,1)} %collective-permute-done.5, bf16[1,4,320,192]{2,3,1,0:T(8,128)(2,1)S(1)} %fusion.43, bf16[1,2,320,192]{2,3,1,0:T(8,128)(2,1)S(1)} %collective-permute-done.4), kind=kLoop, calls=%fused_computation.19 | loop fusion | flops 4915200 | bytes 1977088 | tf_op jit(solution)/shard_map/convert_element_type | solution.py:36
  67.2 0.5 fusion.59
  67.8 0.5 fusion.57
  68.3 0.5 fusion.55
  68.8 0.5 fusion.53
  70.5 0.5 fusion.61
  71.0 1.2 %fusion.24 = (f32[6,320]{1,0:T(8,128)S(1)}, bf16[6,320,192]{1,2,0:T(8,128)(2,1)S(1)}) fusion(bf16[1,8,320,192]{2,3,1,0:T(8,128)(2,1)S(1)} %fusion.15, bf16[3,3,192,192]{2,3,1,0:T(8,128)(2,1)S(1)} %bitcast.419, f32[6,320,192]{1,2,0:T(8,128)S(1)} %fusion.46, f32[6,320,192]{1,2,0:T(8,128)S(1)} %fusion.53, f32[6,320,192]{1,2,0:T(8,128)S(1)} %fusion.55, ...), kind=kOutput, calls=%fused_computation.32 | convolution fusion | flops 146348160 | bytes 16179200 | tf_op jit(solution)/shard_map/frwc,cd->frwd/dot_general | solution.py:47
  72.2 0.6 fusion.44
  72.8 0.4 fusion.96
  75.9 0.4 add_convert_fusion
  76.4 2.4 %collective-permute-start.7 = (bf16[1,4,320,192]{2,3,1,0:T(8,128)(2,1)S(1)}, bf16[1,4,320,192]{2,3,1,0:T(8,128)(2,1)S(1)}, u32[]{:S(2)}, u32[]{:S(2)}) collective-permute-start(bf16[1,4,320,192]{2,3,1,0:T(8,128)(2,1)S(1)} %add_convert_fusion), channel_id=1, source_target_pairs={{0,8},{4,12},{8,16},{12,20},{16,24},{20,28},{1,9},{5,13},{9,17},{1... | collective-permute-start | bytes 1474568 | tf_op jit(solution)/shard_map/ppermute | solution.py:12
  78.7 1.9 %collective-permute-start.6 = (bf16[1,4,320,192]{2,3,1,0:T(8,128)(2,1)S(1)}, bf16[1,4,320,192]{2,3,1,0:T(8,128)(2,1)S(1)}, u32[]{:S(2)}, u32[]{:S(2)}) collective-permute-start(bf16[1,4,320,192]{2,3,1,0:T(8,128)(2,1)S(1)} %add_convert_fusion), channel_id=1, source_target_pairs={{0,4},{4,8},{8,12},{12,16},{16,20},{20,24},{24,28},{1,5},{5,9},{9,... | collective-permute-start | bytes 1474568 | tf_op jit(solution)/shard_map/ppermute | solution.py:12
  81.0 14.3 %collective-permute-done.7 = bf16[1,4,320,192]{2,3,1,0:T(8,128)(2,1)S(1)} collective-permute-done((bf16[1,4,320,192]{2,3,1,0:T(8,128)(2,1)S(1)}, bf16[1,4,320,192]{2,3,1,0:T(8,128)(2,1)S(1)}, u32[]{:S(2)}, u32[]{:S(2)}) %collective-permute-start.7) | collective-permute-done | bytes 491552 | tf_op jit(solution)/shard_map/ppermute | solution.py:12
  95.7 2.1 %collective-permute-done.6 = bf16[1,4,320,192]{2,3,1,0:T(8,128)(2,1)S(1)} collective-permute-done((bf16[1,4,320,192]{2,3,1,0:T(8,128)(2,1)S(1)}, bf16[1,4,320,192]{2,3,1,0:T(8,128)(2,1)S(1)}, u32[]{:S(2)}, u32[]{:S(2)}) %collective-permute-start.6) | collective-permute-done | bytes 491552 | tf_op jit(solution)/shard_map/ppermute | solution.py:12
  97.8 1.2 %fusion.42 = bf16[1,4,320,192]{2,3,1,0:T(8,128)(2,1)} fusion(f32[1,4,320,192]{2,3,1,0:T(8,128)S(1)} %convolution_bitcast_fusion, f32[1,4,320,192]{2,3,1,0:T(8,128)S(1)} %fusion.37, bf16[1,4,320,192]{2,3,1,0:T(8,128)(2,1)S(1)} %collective-permute-done.6, bf16[2,3,192,192]{3,2,1,0:T(8,128)(2,1)S(1)} %copy-done.3), kind=kOutput, calls=%fused_computation.74 | convolution fusion | flops 95109120 | bytes 3538944 | tf_op jit(solution)/shard_map/frwc,cd->frwd/dot_general | solution.py:88
  (39 shorter events, 8.0 us)
Async XLA Ops:
  1.9 11.9 %collective-permute-start = (bf16[1,2,320,192]{2,3,1,0:T(8,128)(2,1)}, bf16[1,2,320,192]{2,3,1,0:T(8,128)(2,1)S(1)}, u32[]{:S(2)}, u32[]{:S(2)}) collective-permute-start(bf16[1,2,320,192]{2,3,1,0:T(8,128)(2,1)} %get-tuple-element.11), channel_id=1, source_target_pairs={{0,1},{1,2},{2,3},{4,5},{5,6},{6,7},{8,9},{9,10},{10,11},{12,13},{... | collective-permute-start | bytes 737288 | tf_op jit(solution)/shard_map/ppermute | solution.py:23
  5.4 10.7 %collective-permute-start.1 = (bf16[1,2,320,192]{2,3,1,0:T(8,128)(2,1)}, bf16[1,2,320,192]{2,3,1,0:T(8,128)(2,1)}, u32[]{:S(2)}, u32[]{:S(2)}) collective-permute-start(bf16[1,2,320,192]{2,3,1,0:T(8,128)(2,1)} %get-tuple-element.12), channel_id=1, source_target_pairs={{1,0},{2,1},{3,2},{5,4},{6,5},{7,6},{9,8},{10,9},{11,10},{13,12},{... | collective-permute-start | bytes 737288 | tf_op jit(solution)/shard_map/ppermute | solution.py:25
  12.1 1.7 %copy-start.4 = (f32[4,192]{1,0:T(4,128)S(1)}, f32[4,192]{1,0:T(4,128)}, u32[]{:S(2)}) copy-start(f32[4,192]{1,0:T(4,128)} %param.6) | copy-start | bytes 9220
  12.1 4.0 %copy-start = (bf16[1,4,320,192]{2,3,1,0:T(8,128)(2,1)S(1)}, bf16[1,4,320,192]{2,3,1,0:T(8,128)(2,1)}, u32[]{:S(2)}) copy-start(bf16[1,4,320,192]{2,3,1,0:T(8,128)(2,1)} %param.4) | copy-start | bytes 1474564
  27.8 5.8 %copy-start.2 = (bf16[2,3,192,192]{3,2,1,0:T(8,128)(2,1)S(1)}, bf16[2,3,192,192]{3,2,1,0:T(8,128)(2,1)}, u32[]{:S(2)}) copy-start(bf16[2,3,192,192]{3,2,1,0:T(8,128)(2,1)} %param.7) | copy-start | bytes 1327108
  28.3 19.0 %collective-permute-start.3 = (bf16[1,4,320,192]{2,3,1,0:T(8,128)(2,1)S(1)}, bf16[1,4,320,192]{2,3,1,0:T(8,128)(2,1)S(1)}, u32[]{:S(2)}, u32[]{:S(2)}) collective-permute-start(bf16[1,4,320,192]{2,3,1,0:T(8,128)(2,1)S(1)} %fusion.41), channel_id=1, source_target_pairs={{0,8},{4,12},{8,16},{12,20},{16,24},{20,28},{1,9},{5,13},{9,17},{1... | collective-permute-start | bytes 1474568 | tf_op jit(solution)/shard_map/ppermute | solution.py:12
  31.7 19.6 %collective-permute-start.2 = (bf16[1,4,320,192]{2,3,1,0:T(8,128)(2,1)S(1)}, bf16[1,4,320,192]{2,3,1,0:T(8,128)(2,1)S(1)}, u32[]{:S(2)}, u32[]{:S(2)}) collective-permute-start(bf16[1,4,320,192]{2,3,1,0:T(8,128)(2,1)S(1)} %fusion.41), channel_id=1, source_target_pairs={{0,4},{4,8},{8,12},{12,16},{16,20},{20,24},{24,28},{1,5},{5,9},{9,... | collective-permute-start | bytes 1474568 | tf_op jit(solution)/shard_map/ppermute | solution.py:12
  51.7 6.9 %copy-start.1 = (bf16[1,3,3,192,192]{4,3,2,1,0:T(8,128)(2,1)S(1)}, bf16[1,3,3,192,192]{4,3,2,1,0:T(8,128)(2,1)}, u32[]{:S(2)}) copy-start(bf16[1,3,3,192,192]{4,3,2,1,0:T(8,128)(2,1)} %get-tuple-element.5) | copy-start | bytes 1990660
  52.6 9.2 %collective-permute-start.4 = (bf16[1,2,320,192]{2,3,1,0:T(8,128)(2,1)}, bf16[1,2,320,192]{2,3,1,0:T(8,128)(2,1)S(1)}, u32[]{:S(2)}, u32[]{:S(2)}) collective-permute-start(bf16[1,2,320,192]{2,3,1,0:T(8,128)(2,1)} %get-tuple-element.9), channel_id=1, source_target_pairs={{0,1},{1,2},{2,3},{4,5},{5,6},{6,7},{8,9},{9,10},{10,11},{12,13},{... | collective-permute-start | bytes 737288 | tf_op jit(solution)/shard_map/ppermute | solution.py:23
  55.1 9.1 %collective-permute-start.5 = (bf16[1,2,320,192]{2,3,1,0:T(8,128)(2,1)}, bf16[1,2,320,192]{2,3,1,0:T(8,128)(2,1)}, u32[]{:S(2)}, u32[]{:S(2)}) collective-permute-start(bf16[1,2,320,192]{2,3,1,0:T(8,128)(2,1)} %get-tuple-element.10), channel_id=1, source_target_pairs={{1,0},{2,1},{3,2},{5,4},{6,5},{7,6},{9,8},{10,9},{11,10},{13,12},{... | collective-permute-start | bytes 737288 | tf_op jit(solution)/shard_map/ppermute | solution.py:25
  75.9 4.7 %copy-start.3 = (bf16[2,3,192,192]{3,2,1,0:T(8,128)(2,1)S(1)}, bf16[2,3,192,192]{3,2,1,0:T(8,128)(2,1)}, u32[]{:S(2)}) copy-start(bf16[2,3,192,192]{3,2,1,0:T(8,128)(2,1)} %param.7) | copy-start | bytes 1327108
  76.4 19.0 %collective-permute-start.7 = (bf16[1,4,320,192]{2,3,1,0:T(8,128)(2,1)S(1)}, bf16[1,4,320,192]{2,3,1,0:T(8,128)(2,1)S(1)}, u32[]{:S(2)}, u32[]{:S(2)}) collective-permute-start(bf16[1,4,320,192]{2,3,1,0:T(8,128)(2,1)S(1)} %add_convert_fusion), channel_id=1, source_target_pairs={{0,8},{4,12},{8,16},{12,20},{16,24},{20,28},{1,9},{5,13},{9,17},{1... | collective-permute-start | bytes 1474568 | tf_op jit(solution)/shard_map/ppermute | solution.py:12
  78.7 19.1 %collective-permute-start.6 = (bf16[1,4,320,192]{2,3,1,0:T(8,128)(2,1)S(1)}, bf16[1,4,320,192]{2,3,1,0:T(8,128)(2,1)S(1)}, u32[]{:S(2)}, u32[]{:S(2)}) collective-permute-start(bf16[1,4,320,192]{2,3,1,0:T(8,128)(2,1)S(1)} %add_convert_fusion), channel_id=1, source_target_pairs={{0,4},{4,8},{8,12},{12,16},{16,20},{20,24},{24,28},{1,5},{5,9},{9,... | collective-permute-start | bytes 1474568 | tf_op jit(solution)/shard_map/ppermute | solution.py:12
where the time goes:
time: 101 us; the launch traced here: 99 us
  waiting for transfers between devices  39.8 us (39%)
  starting transfers between devices  21.4 us (21%)
  matrix products  19.5 us (19%)
  local copies, waits for them, and re-layouts  10.3 us (10%)
  other arithmetic  7.46 us (7%)
    ppermute x4, waiting for transfers between devices, shifted(): return lax.ppermute(block, axis, route)  33.5 us
    dot_general x36, matrix products, convolve(): jnp.einsum('frwc,cd->frwd', window, kernel[row_step, col_step], preferred...  16.7 us
    ppermute x4, starting transfers between devices, shifted(): return lax.ppermute(block, axis, route)  9.6 us
    ppermute x2, starting transfers between devices, extended_2(): lax.ppermute(tail, axis, [(i, (i + 1) % count) for i in range(ends)])  5.97 us
    ppermute x2, starting transfers between devices, extended_2(): lax.ppermute(head, axis, [((i + 1) % count, i) for i in range(ends)])  5.87 us
    convert_element_type x4, other arithmetic, activate(): return jax.nn.silu(scaled).astype(jnp.bfloat16)  4.89 us
    ppermute x2, waiting for transfers between devices, extended_2(): lax.ppermute(head, axis, [((i + 1) % count, i) for i in range(ends)])  4.62 us
    unnamed x14, local copies, waits for them, and re-layouts  3.96 us
  transfers between devices with their start and end apart: 8, of which 7 were waited for; matrix products, arithmetic and copies ran while one was open for 9% of the time, Pallas kernels for 0%

commit v1 on v0

v1 whole, which is shorter than its diff:
```python
import functools

import jax
import jax.numpy as jnp
from jax import lax
from jax.experimental import pallas as pl
from jax.experimental.pallas import tpu as pltpu
from jax.sharding import PartitionSpec as P

epsilon = 1e-06
MESH = pl.DeviceIdType.MESH


def kernel(
    frames,
    strips,
    video_ref,
    weights_ref,
    gains_ref,
    taps_ref,
    out_ref,
    cur,
    act,
    act2,
    inner,
    one_back,
    two_back,
    weights,
    local_sem,
    halo_send,
    halo_recv,
    two_send,
    two_recv,
    one_send,
    one_recv,
):
    f = lax.axis_index("frames")
    z = lax.axis_index("rows")
    blocks, rows, width, channels = inner.shape
    pad = act.shape[-1] // 3
    odd = lax.rem(f, 2)
    even_dev = odd == 0
    pair = f + 1 - 2 * odd
    has_up, has_down = z > 0, z < strips - 1
    has_next, has_prev = f < frames - 2, f > 1
    has_one = f > 0
    gives_one = jnp.logical_or(even_dev, has_prev)

    own = pltpu.make_async_copy(
        video_ref.at[0], cur.at[0, pl.ds(2, rows)], local_sem.at[0]
    )
    own.start()
    loads = []
    for k in range(2 * blocks):
        load = pltpu.make_async_copy(
            weights_ref.at[k],
            weights.at[k, :, :, pl.ds(0, channels), :],
            local_sem.at[1 + k],
        )
        load.start()
        loads.append(load)

    barrier = pltpu.get_barrier_semaphore()
    count = jnp.int32(1)
    pl.semaphore_signal(barrier, inc=1, device_id={"frames": pair}, device_id_type=MESH)
    for present, where in (
        (has_up, {"rows": z - 1}),
        (has_down, {"rows": z + 1}),
        (has_next, {"frames": f + 2}),
        (has_prev, {"frames": f - 2}),
    ):
        count = count + jnp.where(present, 1, 0)

        @pl.when(present)
        def _():
            pl.semaphore_signal(barrier, inc=1, device_id=where, device_id_type=MESH)

    pl.semaphore_wait(barrier, count)

    def up_copy(b, i):
        source = video_ref.at[0, i] if b == 0 else cur.at[b, 2 + i]
        return pltpu.make_async_remote_copy(
            src_ref=source,
            dst_ref=cur.at[b, rows + 2 + i],
            send_sem=halo_send.at[b, 0, i],
            recv_sem=halo_recv.at[b, 0, i],
            device_id={"rows": z - 1},
            device_id_type=MESH,
        )

    def down_copy(b, i):
        source = video_ref.at[0, rows - 2 + i] if b == 0 else cur.at[b, rows + i]
        return pltpu.make_async_remote_copy(
            src_ref=source,
            dst_ref=cur.at[b, i],
            send_sem=halo_send.at[b, 1, i],
            recv_sem=halo_recv.at[b, 1, i],
            device_id={"rows": z + 1},
            device_id_type=MESH,
        )

    def two_copy(b, r):
        return pltpu.make_async_remote_copy(
            src_ref=inner.at[b, r],
            dst_ref=two_back.at[b, r],
            send_sem=two_send.at[b, r],
            recv_sem=two_recv.at[b, r],
            device_id={"frames": f + 2},
            device_id_type=MESH,
        )

    def one_copy(source, b, r):
        return pltpu.make_async_remote_copy(
            src_ref=source.at[b, r],
            dst_ref=one_back.at[b, r],
            send_sem=one_send.at[b, r],
            recv_sem=one_recv.at[b, r],
            device_id={"frames": pair},
            device_id_type=MESH,
        )

    def when(present, action):
        pl.when(present)(action)

    for i in (1, 0):
        when(has_up, lambda: up_copy(0, 1 - i).start())
        when(has_down, lambda: down_copy(0, i).start())

    def clear(ref, b):
        def row(r, carry):
            ref[b, r] = jnp.zeros((width, channels), jnp.bfloat16)
            return carry

        lax.fori_loop(0, rows, row, 0)

    for b in range(blocks):

        @pl.when(jnp.logical_not(has_up))
        def _():
            for i in range(2):
                cur[b, i] = jnp.zeros((width, channels), jnp.bfloat16)

        @pl.when(jnp.logical_not(has_down))
        def _():
            for i in range(2):
                cur[b, rows + 2 + i] = jnp.zeros((width, channels), jnp.bfloat16)

        @pl.when(jnp.logical_not(has_prev))
        def _():
            clear(two_back, b)

        @pl.when(jnp.logical_not(has_one))
        def _():
            clear(one_back, b)

    if pad > channels:

        def clear_pad(buffer, count):
            def row(r, carry):
                for step in range(3):
                    buffer[r, :, step * pad + channels : (step + 1) * pad] = jnp.zeros(
                        (width, pad - channels), jnp.bfloat16
                    )
                return carry

            lax.fori_loop(0, count, row, 0)

        clear_pad(act, rows + 4)
        clear_pad(act2, rows + 2)

        def clear_weights(k, carry):
            for di in range(3):
                for dj in range(3):
                    weights[k, di, dj, channels:pad, :] = jnp.zeros(
                        (pad - channels, channels), jnp.bfloat16
                    )
            return carry

        lax.fori_loop(0, 2 * blocks, clear_weights, 0)

    column = lax.broadcasted_iota(jnp.int32, (width, channels), 0)

    def store_active(buffer, index, values, gain):
        mean_sq = jnp.mean(values * values, axis=-1, keepdims=True)
        half = values * lax.rsqrt(mean_sq + epsilon) * (0.5 * gain)
        active = half + half * jnp.tanh(half)
        before = jnp.where(column == 0, 0.0, pltpu.roll(active, 1, 0))
        after = jnp.where(column == width - 1, 0.0, pltpu.roll(active, width - 1, 0))
        buffer[index, :, 0:channels] = before.astype(jnp.bfloat16)
        buffer[index, :, pad : pad + channels] = active.astype(jnp.bfloat16)
        buffer[index, :, 2 * pad : 2 * pad + channels] = after.astype(jnp.bfloat16)

    def conv_row(buffer, index, k):
        total = None
        for di in range(3):
            term = jnp.dot(
                buffer[index + di],
                weights[k, di].reshape(3 * pad, channels),
                preferred_element_type=jnp.float32,
            )
            total = term if total is None else total + term
        return total

    def loop(count, body):
        def step(i, carry):
            body(i)
            return carry

        lax.fori_loop(0, count, step, 0)

    own.wait()
    for b in range(blocks):
        gain_a = gains_ref[2 * b : 2 * b + 1, :]
        gain_b = gains_ref[2 * b + 1 : 2 * b + 2, :]

        def active_row(index):
            store_active(act, index, cur[b, index].astype(jnp.float32), gain_a)

        def first_row(index, valid=None):
            first = conv_row(act, index, 2 * b)
            if valid is not None:
                first = jnp.where(valid, first, 0.0)
            first = first.astype(jnp.bfloat16).astype(jnp.float32)
            store_active(act2, index, first, gain_b)

        def inner_row(r):
            second = conv_row(act2, r, 2 * b + 1)
            inner[b, r] = (cur[b, 2 + r].astype(jnp.float32) + second).astype(jnp.bfloat16)
            when(has_next, lambda: two_copy(b, r).start())
            when(even_dev, lambda: one_copy(inner, b, r).start())

        loop(rows, lambda i: active_row(2 + i))
        loads[2 * b].wait()
        loop(rows - 2, lambda i: first_row(2 + i))
        when(has_down, lambda: up_copy(b, 0).wait_recv())
        when(has_up, lambda: down_copy(b, 1).wait_recv())
        loop(2, lambda i: active_row(1 + i * (rows + 1)))
        loop(2, lambda i: first_row(1 + i * (rows - 1)))
        loads[2 * b + 1].wait()
        loop(rows - 2, lambda i: inner_row(1 + i))
        when(has_down, lambda: up_copy(b, 1).wait_recv())
        when(has_up, lambda: down_copy(b, 0).wait_recv())
        loop(2, lambda i: active_row(i * (rows + 3)))
        loop(
            2,
            lambda i: first_row(
                i * (rows + 1),
                jnp.where(i == 0, z, strips - 1 - z) > 0,
            ),
        )
        loop(2, lambda i: inner_row(i * (rows - 1)))

        def decode_row(r):
            @pl.when(has_prev)
            def _():
                two_copy(b, r).wait_recv()

                @pl.when(odd == 1)
                def _():
                    one_copy(two_back, b, r).start()

            when(has_one, lambda: one_copy(inner, b, r).wait_recv())
            mine = inner[b, r]
            total = mine.astype(jnp.float32)
            for k, taken in enumerate((mine, one_back[b, r], two_back[b, r])):
                total = total + jnp.dot(
                    taken, taps_ref[b, k], preferred_element_type=jnp.float32
                )
            total = total.astype(jnp.bfloat16)
            if b == blocks - 1:
                out_ref[0, r] = total
            else:
                cur[b + 1, 2 + r] = total

        def share(r):
            if b < blocks - 1:
                if r < 2:
                    when(has_up, lambda: up_copy(b + 1, r).start())
                if r >= rows - 2:
                    when(has_down, lambda: down_copy(b + 1, r - rows + 2).start())

        if b == blocks - 1:
            loop(rows - 2, lambda i: decode_row(1 + i))
            loop(2, lambda i: decode_row(i * (rows - 1)))
        else:
            for r in list(range(1, rows - 1)) + [0, rows - 1]:
                decode_row(r)
                share(r)

    for b in range(blocks):
        for i in range(2):
            when(has_up, lambda: up_copy(b, i).wait_send())
            when(has_down, lambda: down_copy(b, i).wait_send())
        for r in range(rows):
            when(has_next, lambda: two_copy(b, r).wait_send())
            when(gives_one, lambda: one_copy(inner, b, r).wait_send())


def solution(mesh):
    frames, strips = mesh.shape["frames"], mesh.shape["rows"]

    def on_device(video, spatial_weights, norm_gains, temporal_weights):
        held, rows, width, channels = video.shape
        blocks = temporal_weights.shape[0]
        assert held == 1 and rows > 2 and frames % 2 == 0
        pad = -(-channels // 256) * 256
        strip = (blocks, rows, width, channels)
        any_space = pl.BlockSpec(memory_space=pl.ANY)
        vmem = pl.BlockSpec(memory_space=pltpu.VMEM)
        dma = pltpu.SemaphoreType.DMA
        return pl.pallas_call(
            functools.partial(kernel, frames, strips),
            out_shape=jax.ShapeDtypeStruct(video.shape, video.dtype),
            in_specs=[any_space, any_space, vmem, vmem],
            out_specs=vmem,
            scratch_shapes=[
                pltpu.VMEM((blocks, rows + 4, width, channels), jnp.bfloat16),
                pltpu.VMEM((rows + 4, width, 3 * pad), jnp.bfloat16),
                pltpu.VMEM((rows + 2, width, 3 * pad), jnp.bfloat16),
                pltpu.VMEM(strip, jnp.bfloat16),
                pltpu.VMEM(strip, jnp.bfloat16),
                pltpu.VMEM(strip, jnp.bfloat16),
                pltpu.VMEM((2 * blocks, 3, 3, pad, channels), jnp.bfloat16),
                dma((1 + 2 * blocks,)),
                dma((blocks, 2, 2)),
                dma((blocks, 2, 2)),
                dma((blocks, rows)),
                dma((blocks, rows)),
                dma((blocks, rows)),
                dma((blocks, rows)),
            ],
            compiler_params=pltpu.CompilerParams(
                collective_id=0, has_side_effects=True, vmem_limit_bytes=48 << 20
            ),
        )(video, spatial_weights, norm_gains, temporal_weights)

    placed = (P("frames", "rows", None, None), P(), P(), P())
    return jax.shard_map(
        on_device,
        mesh=mesh,
        in_specs=placed,
        out_specs=P("frames", "rows", None, None),
        check_vma=False,
    )
```

time: 101 us -> 52.2 us (0.52); the launches traced: 99 us -> 51.9 us
  Pallas kernels: 0 us -> 45.7 us
  waiting for transfers between devices: 39.8 us -> 0 us
  starting transfers between devices: 21.4 us -> 0 us
  matrix products: 19.5 us -> 0 us
  other arithmetic: 7.46 us -> 0 us
  local copies, waits for them, and re-layouts: 10.3 us -> 6.17 us
    pallas_call x0 -> x1, Pallas kernels: none -> 45.7 us  [on_device(): pl.pallas_call(functools.partial(kernel, frames, strips), out_shape=jax.S...]
    ppermute x8 -> x0, waiting for transfers between devices: 39.8 us -> none  [the longest x4 33.5 us: shifted(): return lax.ppermute(block, axis, route)]
    ppermute x8 -> x0, starting transfers between devices: 21.4 us -> none  [the longest x4 9.6 us: shifted(): return lax.ppermute(block, axis, route)]
    dot_general x42 -> x0, matrix products: 19.5 us -> none  [the longest x36 16.7 us: convolve(): jnp.einsum('frwc,cd->frwd', window, kernel[row_step, col_step], preferred...]
    slice x4 -> x0, local copies, waits for them, and re-layouts: 6.36 us -> none  [the longest x1 3.56 us: on_device(): spatial_weights[2 * block + 1]]
    convert_element_type x4 -> x0, other arithmetic: 4.89 us -> none  [activate(): return jax.nn.silu(scaled).astype(jnp.bfloat16)]
    reduce_sum x2 -> x0, other arithmetic: 2.53 us -> none  [activate(): mean_sq = jnp.mean(values * values, axis=-1, keepdims=True)]
    unnamed x14 -> x7, local copies, waits for them, and re-layouts: 3.96 us -> 5.08 us
  transfers between devices with their start and end apart: 8 -> 0, of which waited for: 7 -> 0; matrix products, arithmetic and copies ran while one was open for 9% -> 0% of each run, Pallas kernels for 0% -> 0%
where the time goes in v1:
time: 52.2 us; the launch traced here: 51.9 us
  Pallas kernels  45.7 us (88%)
  local copies, waits for them, and re-layouts  6.17 us (12%)
    pallas_call x1, Pallas kernels, on_device(): pl.pallas_call(functools.partial(kernel, frames, strips), out_shape=jax.S...  45.7 us
    unnamed x7, local copies, waits for them, and re-layouts  5.08 us
    pallas_call x1, local copies, waits for them, and re-layouts, on_device(): pl.pallas_call(functools.partial(kernel, frames, strips), out_shape=jax.S...  1.09 us

profile of v1, /device:TPU:20, one launch (start us, length us, event | category | flops | bytes accessed | tf_op | source)
XLA Modules:
  0.0 51.9 jit_solution(6604740849742378291)
XLA Ops:
  0.0 1.3 %copy.5.video_ref = bf16[1,4,320,192]{3,2,1,0:T(8,128)(2,1)S(1)} copy(bf16[1,4,320,192]{2,3,1,0:T(8,128)(2,1)} %param.4) | data formatting | bytes 983040 | tf_op args[0]
  1.3 0.0 copy-start
  1.3 2.0 %copy-done = bf16[4,3,3,192,192]{4,3,2,1,0:T(8,128)(2,1)S(1)} copy-done((bf16[4,3,3,192,192]{4,3,2,1,0:T(8,128)(2,1)S(1)}, bf16[4,3,3,192,192]{4,3,2,1,0:T(8,128)(2,1)}, u32[]{:S(2)}) %copy-start) | copy-done | bytes 2654232
  3.3 0.0 copy-start.1
  3.3 1.1 %copy-done.1 = bf16[2,3,192,192]{3,2,1,0:T(8,128)(2,1)S(1)} copy-done((bf16[2,3,192,192]{3,2,1,0:T(8,128)(2,1)S(1)}, bf16[2,3,192,192]{3,2,1,0:T(8,128)(2,1)}, u32[]{:S(2)}) %copy-start.1) | copy-done | bytes 442392
  4.4 0.0 copy-start.2
  4.4 0.7 %copy-done.2 = f32[4,192]{1,0:T(4,128)S(1)} copy-done((f32[4,192]{1,0:T(4,128)S(1)}, f32[4,192]{1,0:T(4,128)}, u32[]{:S(2)}) %copy-start.2) | copy-done | bytes 3096
  5.1 45.7 %shard_map.46 = bf16[1,4,320,192]{3,2,1,0:T(8,128)(2,1)S(1)} custom-call(bf16[1,4,320,192]{3,2,1,0:T(8,128)(2,1)S(1)} %copy.5.video_ref, bf16[4,3,3,192,192]{4,3,2,1,0:T(8,128)(2,1)S(1)} %copy-done, f32[4,192]{1,0:T(4,128)S(1)} %copy-done.2, bf16[2,3,192,192]{3,2,1,0:T(8,128)(2,1)S(1)} %copy-done.1), custom_call_target="tpu_custom_call" | custom-call | tf_op jit(solution)/shard_map/pallas_call | solution.py:311
  50.8 1.1 %copy.6 = bf16[1,4,320,192]{2,3,1,0:T(8,128)(2,1)} copy(bf16[1,4,320,192]{3,2,1,0:T(8,128)(2,1)S(1)} %shard_map.46) | data formatting | bytes 983040 | tf_op jit(solution)/shard_map/pallas_call | solution.py:311
Async XLA Ops:
  1.3 2.0 %copy-start = (bf16[4,3,3,192,192]{4,3,2,1,0:T(8,128)(2,1)S(1)}, bf16[4,3,3,192,192]{4,3,2,1,0:T(8,128)(2,1)}, u32[]{:S(2)}) copy-start(bf16[4,3,3,192,192]{4,3,2,1,0:T(8,128)(2,1)} %weights_ref.1) | copy-start | bytes 7962628
  3.3 1.1 %copy-start.1 = (bf16[2,3,192,192]{3,2,1,0:T(8,128)(2,1)S(1)}, bf16[2,3,192,192]{3,2,1,0:T(8,128)(2,1)}, u32[]{:S(2)}) copy-start(bf16[2,3,192,192]{3,2,1,0:T(8,128)(2,1)} %taps_ref.1) | copy-start | bytes 1327108
  4.4 0.7 %copy-start.2 = (f32[4,192]{1,0:T(4,128)S(1)}, f32[4,192]{1,0:T(4,128)}, u32[]{:S(2)}) copy-start(f32[4,192]{1,0:T(4,128)} %gains_ref.1) | copy-start | bytes 9220

commit v2 on v1

--- a/solution.py
+++ b/solution.py
@@ -23,10 +23,14 @@
     act,
     act2,
     inner,
+    packed,
     one_back,
     two_back,
     weights,
+    gains,
+    taps,
     local_sem,
+    small_sem,
     halo_send,
     halo_recv,
     two_send,
@@ -38,6 +42,8 @@
     z = lax.axis_index("rows")
     blocks, rows, width, channels = inner.shape
     pad = act.shape[-1] // 3
+    lanes = packed.shape[-1]
+    middle = width // 2
     odd = lax.rem(f, 2)
     even_dev = odd == 0
     pair = f + 1 - 2 * odd
@@ -60,6 +66,11 @@
         load.start()
         loads.append(load)
 
+    gains_load = pltpu.make_async_copy(gains_ref, gains, small_sem.at[0])
+    gains_load.start()
+    taps_load = pltpu.make_async_copy(taps_ref, taps, small_sem.at[1])
+    taps_load.start()
+
     barrier = pltpu.get_barrier_semaphore()
     count = jnp.int32(1)
     pl.semaphore_signal(barrier, inc=1, device_id={"frames": pair}, device_id_type=MESH)
@@ -101,7 +112,7 @@
 
     def two_copy(b, r):
         return pltpu.make_async_remote_copy(
-            src_ref=inner.at[b, r],
+            src_ref=packed.at[b, r],
             dst_ref=two_back.at[b, r],
             send_sem=two_send.at[b, r],
             recv_sem=two_recv.at[b, r],
@@ -128,7 +139,7 @@
 
     def clear(ref, b):
         def row(r, carry):
-            ref[b, r] = jnp.zeros((width, channels), jnp.bfloat16)
+            ref[b, r] = jnp.zeros(ref.shape[2:], jnp.bfloat16)
             return carry
 
         lax.fori_loop(0, rows, row, 0)
@@ -209,9 +220,10 @@
         lax.fori_loop(0, count, step, 0)
 
     own.wait()
+    gains_load.wait()
     for b in range(blocks):
-        gain_a = gains_ref[2 * b : 2 * b + 1, :]
-        gain_b = gains_ref[2 * b + 1 : 2 * b + 2, :]
+        gain_a = gains[2 * b : 2 * b + 1, :]
+        gain_b = gains[2 * b + 1 : 2 * b + 2, :]
 
         def active_row(index):
             store_active(act, index, cur[b, index].astype(jnp.float32), gain_a)
@@ -225,9 +237,15 @@
 
         def inner_row(r):
             second = conv_row(act2, r, 2 * b + 1)
-            inner[b, r] = (cur[b, 2 + r].astype(jnp.float32) + second).astype(jnp.bfloat16)
+            value = cur[b, 2 + r].astype(jnp.float32) + second
+            inner[b, r] = value.astype(jnp.bfloat16)
+            packed[b, r, 0:width, :] = value[:, 0:lanes].astype(jnp.bfloat16)
+            rest = value[:, lanes:channels]
+            packed[b, r, width : width + middle, :] = jnp.concatenate(
+                [rest[0:middle], rest[middle:width]], axis=1
+            ).astype(jnp.bfloat16)
             when(has_next, lambda: two_copy(b, r).start())
-            when(even_dev, lambda: one_copy(inner, b, r).start())
+            when(even_dev, lambda: one_copy(packed, b, r).start())
 
         loop(rows, lambda i: active_row(2 + i))
         loads[2 * b].wait()
@@ -250,6 +268,9 @@
         )
         loop(2, lambda i: inner_row(i * (rows - 1)))
 
+        if b == 0:
+            taps_load.wait()
+
         def decode_row(r):
             @pl.when(has_prev)
             def _():
@@ -259,13 +280,30 @@
                 def _():
                     one_copy(two_back, b, r).start()
 
-            when(has_one, lambda: one_copy(inner, b, r).wait_recv())
+            when(has_one, lambda: one_copy(packed, b, r).wait_recv())
             mine = inner[b, r]
             total = mine.astype(jnp.float32)
-            for k, taken in enumerate((mine, one_back[b, r], two_back[b, r])):
+            total = total + jnp.dot(
+                mine, taps[b, 0], preferred_element_type=jnp.float32
+            )
+            for k, back in ((1, one_back), (2, two_back)):
                 total = total + jnp.dot(
-                    taken, taps_ref[b, k], preferred_element_type=jnp.float32
+                    back[b, r, 0:width, :],
+                    taps[b, k, 0:lanes, :],
+                    preferred_element_type=jnp.float32,
                 )
+                rest = back[b, r, width : width + middle, :]
+                tap = taps[b, k, lanes:channels, :]
+                blank = jnp.zeros_like(tap)
+                halves = [
+                    jnp.dot(
+                        rest,
+                        jnp.concatenate(side, axis=0),
+                        preferred_element_type=jnp.float32,
+                    )
+                    for side in ([tap, blank], [blank, tap])
+                ]
+                total = total + jnp.concatenate(halves, axis=0)
             total = total.astype(jnp.bfloat16)
             if b == blocks - 1:
                 out_ref[0, r] = total
@@ -293,7 +331,7 @@
             when(has_down, lambda: down_copy(b, i).wait_send())
         for r in range(rows):
             when(has_next, lambda: two_copy(b, r).wait_send())
-            when(gives_one, lambda: one_copy(inner, b, r).wait_send())
+            when(gives_one, lambda: one_copy(packed, b, r).wait_send())
 
 
 def solution(mesh):
@@ -305,23 +343,30 @@
         assert held == 1 and rows > 2 and frames % 2 == 0
         pad = -(-channels // 256) * 256
         strip = (blocks, rows, width, channels)
-        any_space = pl.BlockSpec(memory_space=pl.ANY)
+        lanes = channels * 2 // 3
+        assert 2 * (channels - lanes) == lanes
+        sent = (blocks, rows, width + width // 2, lanes)
+        any_space = pl.BlockSpec(memory_space=pltpu.HBM)
         vmem = pl.BlockSpec(memory_space=pltpu.VMEM)
         dma = pltpu.SemaphoreType.DMA
         return pl.pallas_call(
             functools.partial(kernel, frames, strips),
             out_shape=jax.ShapeDtypeStruct(video.shape, video.dtype),
-            in_specs=[any_space, any_space, vmem, vmem],
+            in_specs=[any_space] * 4,
             out_specs=vmem,
             scratch_shapes=[
                 pltpu.VMEM((blocks, rows + 4, width, channels), jnp.bfloat16),
                 pltpu.VMEM((rows + 4, width, 3 * pad), jnp.bfloat16),
                 pltpu.VMEM((rows + 2, width, 3 * pad), jnp.bfloat16),
                 pltpu.VMEM(strip, jnp.bfloat16),
-                pltpu.VMEM(strip, jnp.bfloat16),
-                pltpu.VMEM(strip, jnp.bfloat16),
+                pltpu.VMEM(sent, jnp.bfloat16),
+                pltpu.VMEM(sent, jnp.bfloat16),
+                pltpu.VMEM(sent, jnp.bfloat16),
                 pltpu.VMEM((2 * blocks, 3, 3, pad, channels), jnp.bfloat16),
+                pltpu.VMEM(norm_gains.shape, jnp.float32),
+                pltpu.VMEM(temporal_weights.shape, jnp.bfloat16),
                 dma((1 + 2 * blocks,)),
+                dma((2,)),
                 dma((blocks, 2, 2)),
                 dma((blocks, 2, 2)),
                 dma((blocks, rows)),
@@ -330,7 +375,7 @@
                 dma((blocks, rows)),
             ],
             compiler_params=pltpu.CompilerParams(
-                collective_id=0, has_side_effects=True, vmem_limit_bytes=48 << 20
+                collective_id=0, has_side_effects=True, vmem_limit_bytes=67043328
             ),
         )(video, spatial_weights, norm_gains, temporal_weights)
 

time: 52.2 us -> 45.5 us (0.87)
  Pallas kernels: 45.7 us -> 41 us
  local copies, waits for them, and re-layouts: 6.17 us -> 4.35 us
    pallas_call x1, Pallas kernels: 45.7 us -> 41 us  [on_device(): pl.pallas_call(functools.partial(kernel, frames, strips), out_shape=jax.S...]
    unnamed x7 -> x1, local copies, waits for them, and re-layouts: 5.08 us -> 2.17 us
    pallas_call x1, local copies, waits for them, and re-layouts: 1.09 us -> 2.18 us  [on_device(): pl.pallas_call(functools.partial(kernel, frames, strips), out_shape=jax.S...]
where the time goes in v2:
time: 45.5 us; the launch traced here: 45.3 us
  Pallas kernels  41 us (90%)
  local copies, waits for them, and re-layouts  4.35 us (10%)
    pallas_call x1, Pallas kernels, on_device(): pl.pallas_call(functools.partial(kernel, frames, strips), out_shape=jax.S...  41 us
    pallas_call x1, local copies, waits for them, and re-layouts, on_device(): pl.pallas_call(functools.partial(kernel, frames, strips), out_shape=jax.S...  2.18 us
    unnamed x1, local copies, waits for them, and re-layouts  2.17 us

profile of v2, /device:TPU:20, one launch (start us, length us, event | category | flops | bytes accessed | tf_op | source)
XLA Modules:
  0.0 45.3 jit_solution(1389346199842895610)
XLA Ops:
  0.0 2.2 %copy.5.video_ref = bf16[1,4,320,192]{3,2,1,0:T(8,128)(2,1)} copy(bf16[1,4,320,192]{2,3,1,0:T(8,128)(2,1)} %param.4) | data formatting | bytes 983040 | tf_op args[0]
  2.2 41.0 %shard_map.46 = bf16[1,4,320,192]{3,2,1,0:T(8,128)(2,1)} custom-call(bf16[1,4,320,192]{3,2,1,0:T(8,128)(2,1)} %copy.5.video_ref, bf16[4,3,3,192,192]{4,3,2,1,0:T(8,128)(2,1)} %weights_ref.1, f32[4,192]{1,0:T(4,128)} %gains_ref.1, bf16[2,3,192,192]{3,2,1,0:T(8,128)(2,1)} %taps_ref.1), custom_call_target="tpu_custom_call" | custom-call | tf_op jit(solution)/shard_map/pallas_call | solution.py:352
  43.2 2.2 %copy.6 = bf16[1,4,320,192]{2,3,1,0:T(8,128)(2,1)} copy(bf16[1,4,320,192]{3,2,1,0:T(8,128)(2,1)} %shard_map.46) | data formatting | bytes 983040 | tf_op jit(solution)/shard_map/pallas_call | solution.py:352
